TPU v7x, 512 devices: a whole 4x4x16 slice. The times are simulated.
512 devices in a mesh: term: 32 (over z, core), row: 16 (over x, y).
Axes of the slice: x: 4, y: 4, z: 16, core: 2. Of those that a mesh axis runs over, the one named last changes fastest.
Arguments:
- psi: bfloat16 [2048, 2048], P('row'), may hold values from -6 to 6
- left_ops: bfloat16 [32, 2048, 2048], P('term', 'row'), may hold values from -0.0234375 to 0.0234375
- right_ops: bfloat16 [32, 2048, 2048], P('term', 'row'), may hold values from -0.25 to 0.25
- block_mask: int32 [32, 16, 16], P('term', 'row'), may hold values from 0 to 1, as said below
Outputs:
- sigma: bfloat16 [2048, 2048], P('row', 'term')
Inputs may be any that keep to these rules, and one draw needn't show every extreme that they name: Entries are 0 or 1; block_mask[t, i, i] = 1 for every term and block.
All inputs are finite; a program needn't handle non-finite values.
Results may differ from a plain program's by a relative error of at most 0.0049.
Values may be sent and summed in bfloat16 or wider, within the bound.
A program may use at most 64 MiB of HBM per device.

v0:
```python
import jax
import jax.numpy as jnp
from jax import lax
from jax.sharding import PartitionSpec as P


def swapped(value, axis, bit):
    mask = 2**bit
    pairs = [(source, source ^ mask) for source in range(lax.axis_size(axis))]
    return lax.ppermute(value, axis, pairs)


def split_up(array, dim, size):
    shape = array.shape
    parts = array.reshape(*shape[:dim], size, shape[dim] // size, *shape[dim + 1 :])
    return jnp.moveaxis(parts, dim, 0)


def summed_on_arrival(array, axis, dim):
    size = lax.axis_size(axis)
    parts = lax.all_to_all(split_up(array, dim, size), axis, 0, 0, tiled=True)
    return jnp.sum(parts, axis=0)


def make_fold(operands, piece):
    outputs = []
    for member in range(operands.shape[0]):
        columns = operands[member]
        outputs.append(jnp.dot(columns, piece, preferred_element_type=jnp.float32))
    return jnp.stack(outputs)


def shards(psi, left_ops, right_ops, block_mask):
    rows = psi.shape[0]
    width = psi.shape[1]
    local_terms = left_ops.shape[0]
    row_blocks = block_mask.shape[1]
    col_blocks = block_mask.shape[2]
    blk = width // col_blocks
    grid = jnp.broadcast_to(
        block_mask[:, :, None, :, None], (local_terms, row_blocks, blk, col_blocks, blk)
    )
    masked = left_ops * grid.reshape(local_terms, rows, width).astype(jnp.bfloat16)
    half = width // 2
    side = lax.axis_index("term") % 2
    own_cols = lax.dynamic_slice_in_dim(psi, side * half, half, 1)
    keep_right = lax.dynamic_slice_in_dim(right_ops, side * half, half, 2)
    give_right = lax.dynamic_slice_in_dim(right_ops, (1 - side) * half, half, 2)
    partner_masked, partner_right, partner_mask = swapped(
        (masked, give_right, block_mask.astype(jnp.bfloat16)), "term", 0
    )
    operands = jnp.concatenate([masked, partner_masked], 0)
    inner = make_fold(operands, lax.all_gather(own_cols, "row", axis=0, tiled=True))
    inner = inner.astype(jnp.bfloat16)
    both_right = jnp.concatenate([keep_right, partner_right], 0)
    partial_value = jnp.einsum(
        "kih,kah->ia",
        inner,
        lax.all_gather(both_right, "row", axis=1, tiled=True),
        preferred_element_type=jnp.float32,
    )
    return summed_on_arrival(partial_value, "term", 1).astype(jnp.bfloat16)


def solution(mesh):
    in_specs = (
        P("row", None),
        P("term", "row", None),
        P("term", "row", None),
        P("term", "row", None),
    )
    out_specs = P("row", "term")
    return jax.shard_map(shards, mesh=mesh, in_specs=in_specs, out_specs=out_specs, check_vma=False)
```

profile of v0, /device:TPU:1, one launch (start us, length us, event | category | flops | bytes accessed | tf_op | source)
XLA Modules:
  0.0 253.2 jit_solution(4638566160298173793)
XLA Ops:
  6.5 0.0 copy-start
  6.5 0.0 all-gather.3.cloned.1.call-start
  6.5 1.0 copy-done
  7.6 0.7 constant_dynamic-slice_fusion.2
  8.3 0.0 all-gather.3.cloned.1.call-update
  8.3 0.0 all-gather.5.cloned.1.call-start
  8.4 1.1 constant_dynamic-slice_fusion.1
  9.5 8.7 %collective-permute-start.1 = (bf16[1,128,1024]{2,1,0:T(8,128)(2,1)S(1)}, bf16[1,128,1024]{2,1,0:T(8,128)(2,1)S(1)}, u32[]{:S(2)}, u32[]{:S(2)}) collective-permute-start(bf16[1,128,1024]{2,1,0:T(8,128)(2,1)S(1)} %get-tuple-element.6), channel_id=1, source_target_pairs={{0,16},{16,0},{32,48},{48,32},{64,80},{80,64},{96,112},{112,96},{1... | collective-permute-start | bytes 786440 | tf_op jit(solution)/shard_map/ppermute | solution.py:10
  18.2 1.1 collective-permute-done.1
  19.4 0.9 pad_maximum_fusion
  20.2 0.0 all-gather.5.cloned.1.call-update
  20.3 0.7 convert_bitcast_fusion
  20.9 0.1 broadcast_bitcast_fusion
  21.0 1.1 broadcast_multiply_fusion
  22.1 2.3 collective-permute-start
  24.4 57.9 %all-gather.3.cloned.1.call-done = bf16[2048,1024]{1,0:T(8,128)(2,1)} async-done(((bf16[128,1024]{1,0:T(8,128)(2,1)}), bf16[2048,1024]{1,0:T(8,128)(2,1)}) %all-gather.3.cloned.1.call-update) | async-done | bytes 4194320 | tf_op jit(solution)/shard_map/all_gather | solution.py:53
  82.2 0.0 copy-start.1
  82.2 3.1 %fusion = bf16[1,128,1024]{2,1,0:T(8,128)(2,1)S(1)} fusion(bf16[2048,1024]{1,0:T(8,128)(2,1)} %all-gather.3.cloned.1.call-done, bf16[1,128,2048]{2,1,0:T(8,128)(2,1)S(1)} %broadcast_multiply_fusion), kind=kOutput, calls=%fused_computation.2 | convolution fusion | flops 537001984 | bytes 4980736 | tf_op jit(solution)/shard_map/dot_general | solution.py:29
  85.3 0.0 collective-permute-done
  85.3 0.4 copy-done.1
  85.7 0.7 fusion.1
  86.4 84.8 %all-gather.5.cloned.1.call-done = bf16[2,2048,1024]{2,1,0:T(8,128)(2,1)} async-done(((bf16[2,128,1024]{2,1,0:T(8,128)(2,1)}), bf16[2,2048,1024]{2,1,0:T(8,128)(2,1)}) %all-gather.5.cloned.1.call-update) | async-done | bytes 8388624 | tf_op jit(solution)/shard_map/all_gather | solution.py:59
  171.2 5.8 %fusion.2 = f32[128,2048,1]{0,1,2:T(8,128)S(1)} fusion(bf16[2,2048,1024]{2,1,0:T(8,128)(2,1)} %all-gather.5.cloned.1.call-done, bf16[1,128,1024]{2,1,0:T(8,128)(2,1)S(1)} %fusion.1, bf16[1,128,1024]{2,1,0:T(8,128)(2,1)S(1)} %fusion), kind=kOutput, calls=%fused_computation.4 | convolution fusion | flops 1074003968 | bytes 9961472 | tf_op jit(solution)/shard_map/kih,kah->ia/dot_general | solution.py:56
  177.0 68.6 %all_to_all.5 = f32[32,128,64]{1,2,0:T(8,128)S(1)} all-to-all(f32[32,128,64]{1,2,0:T(8,128)S(1)} %bitcast.22), channel_id=1, replica_groups=mesh['term'=32,'row'=16] {'term'}, dimensions={0} | all-to-all | bytes 2097152 | tf_op jit(solution)/shard_map/all_to_all | solution.py:21
  245.7 0.7 reduce_sum.9
Async XLA Ops:
  6.5 1.0 copy-start
  6.5 75.7 %all-gather.3.cloned.1.call-start = ((), (), s32[]{:S(2)}) async-start(), calls=%async_computation.1 | async-start | bytes 4456448 | tf_op jit(solution)/shard_map/all_gather | solution.py:53
  8.3 162.9 %all-gather.5.cloned.1.call-start = ((), (), s32[]{:S(2)}) async-start(), calls=%async_computation.2 | async-start | bytes 8912896 | tf_op jit(solution)/shard_map/all_gather | solution.py:59
  9.5 9.9 %collective-permute-start.1 = (bf16[1,128,1024]{2,1,0:T(8,128)(2,1)S(1)}, bf16[1,128,1024]{2,1,0:T(8,128)(2,1)S(1)}, u32[]{:S(2)}, u32[]{:S(2)}) collective-permute-start(bf16[1,128,1024]{2,1,0:T(8,128)(2,1)S(1)} %get-tuple-element.6), channel_id=1, source_target_pairs={{0,16},{16,0},{32,48},{48,32},{64,80},{80,64},{96,112},{112,96},{1... | collective-permute-start | bytes 786440 | tf_op jit(solution)/shard_map/ppermute | solution.py:10
  22.1 63.2 %collective-permute-start = (bf16[1,128,2048]{2,1,0:T(8,128)(2,1)S(1)}, bf16[1,128,2048]{2,1,0:T(8,128)(2,1)S(1)}, u32[]{:S(2)}, u32[]{:S(2)}) collective-permute-start(bf16[1,128,2048]{2,1,0:T(8,128)(2,1)S(1)} %broadcast_multiply_fusion), channel_id=1, source_target_pairs={{0,16},{16,0},{32,48},{48,32},{64,80},{80,64},{96,112},{112,96},{1... | collective-permute-start | bytes 1572872 | tf_op jit(solution)/shard_map/ppermute | solution.py:10
  82.2 3.4 %copy-start.1 = (bf16[2048,1024]{1,0:T(8,128)(2,1)S(1)}, bf16[2048,1024]{1,0:T(8,128)(2,1)}, u32[]{:S(2)}) copy-start(bf16[2048,1024]{1,0:T(8,128)(2,1)} %all-gather.3.cloned.1.call-done) | copy-start | bytes 12582916
Sparse Core Ops, SparseCore 0:
  10.3 71.8 all-gather.2
  85.3 85.8 all-gather.4
where the time goes:
time: 254 us; the launch traced here: 253 us
  waiting for transfers between devices  144 us (57%)
  blocking collectives  68.6 us (27%)
  between operations  13.5 us (5%)
  starting transfers between devices  11.1 us (4%)
  matrix products  9.58 us (4%)
  local copies, waits for them, and re-layouts  3.29 us (1%)
  other arithmetic  3.29 us (1%)
    all_gather x1, waiting for transfers between devices, shards(): lax.all_gather(both_right, 'row', axis=1, tiled=True)  84.8 us
    all_to_all x1, blocking collectives, summed_on_arrival(): parts = lax.all_to_all(split_up(array, dim, size), axis, 0, 0, tiled=True)  68.6 us
    all_gather x1, waiting for transfers between devices, shards(): lax.all_gather(own_cols, 'row', axis=0, tiled=True)  57.9 us
    ppermute x2, starting transfers between devices, swapped(): return lax.ppermute(value, axis, pairs)  11 us
    dot_general x1, matrix products, shards(): jnp.einsum('kih,kah->ia', inner, lax.all_gather(both_right, 'row', axis=1...  5.78 us
  transfers between devices with their start and end apart: 4, of which 3 were waited for; matrix products, arithmetic and copies ran while one was open for 3% of the time, Pallas kernels for 0%

commit v1 on v0

v1 whole, which is shorter than its diff:
```python
import jax
import jax.numpy as jnp
from jax import lax
from jax.experimental import pallas as pl
from jax.experimental.pallas import tpu as pltpu
from jax.sharding import PartitionSpec as P

MESH = pl.DeviceIdType.MESH
N = 4
NZ = 16
B = 128
CH = 32
W = 2048
F32 = jnp.float32
BF16 = jnp.bfloat16


def dot_nt(a, b):
    return lax.dot_general(a, b, (((1,), (1,)), ((), ())), preferred_element_type=F32)


def kernel(
    psi, left, right, mask, out,
    p_buf, r_buf, m_buf, l_buf, q_buf, s_buf, e_buf, t_buf, g_buf,
    load_sem, rs, rr, ps, pr, fs, ms, mr, qs, qr, es, er, zs, zr, hs,
):
    t = lax.axis_index("term")
    row = lax.axis_index("row")
    z, c = t // 2, t % 2
    x, y = row // N, row % N
    xl, xr, xo = (x + 3) % N, (x + 1) % N, (x + 2) % N
    yl, yr, yo = (y + 3) % N, (y + 1) % N, (y + 2) % N
    to_xl, to_xr = (t, xl * N + y), (t, xr * N + y)
    to_yl, to_yr = (t, x * N + yl), (t, x * N + yr)
    twin = (z * 2 + 1 - c, row)

    def along_z(step):
        return (((z + step + NZ) % NZ) * 2 + c, row)

    sent = []

    def send(src, dst, ssem, rsem, device):
        copy = pltpu.make_async_remote_copy(
            src_ref=src, dst_ref=dst, send_sem=ssem, recv_sem=rsem, device_id=device, device_id_type=MESH
        )
        copy.start()
        sent.append(copy)

    def arrived(dst, rsem):
        pltpu.make_async_remote_copy(
            src_ref=dst, dst_ref=dst, send_sem=rsem, recv_sem=rsem, device_id=twin, device_id_type=MESH
        ).wait_recv()

    load_r = pltpu.make_async_copy(right.at[0], r_buf.at[x], load_sem.at[0])
    load_p = pltpu.make_async_copy(psi, p_buf.at[y], load_sem.at[1])
    load_l = pltpu.make_async_copy(left.at[0], l_buf, load_sem.at[2])
    load_l.start()
    load_p.start()
    load_r.start()

    barrier = pltpu.get_barrier_semaphore()
    peers = [to_xl, to_xr, twin, along_z(1), along_z(-1)]
    for other in (yl, yr, yo):
        peers += [(t, x * N + other), (z * 2 + 1 - c, x * N + other)]
    for peer in peers:
        pl.semaphore_signal(barrier, inc=1, device_id=peer, device_id_type=MESH)

    load_l.wait()
    for k in range(W // B):
        scale = jnp.full((B, B), mask[0, 0, k].astype(F32), F32).astype(BF16)
        m_buf[y, :, k * B : (k + 1) * B] = l_buf[:, k * B : (k + 1) * B] * scale

    pl.semaphore_wait(barrier, len(peers))

    def greet(k, distance):
        pl.semaphore_signal(hs.at[k, 0], inc=1, device_id=along_z(distance), device_id_type=MESH)
        if 2 * distance < NZ:
            pl.semaphore_signal(hs.at[k, 1], inc=1, device_id=along_z(-distance), device_id_type=MESH)

    def greeted(k, distance):
        pl.semaphore_wait(hs.at[k, 0], 1)
        if 2 * distance < NZ:
            pl.semaphore_wait(hs.at[k, 1], 1)

    def rows(k):
        return pl.ds(k * CH, CH)

    greet(0, 1)
    lo = 2 * c
    for step in range(4):
        ahead, back = step, (step + 2) % 4
        send(right.at[0, rows(ahead)], r_buf.at[x, rows(ahead)], rs.at[0, step], rr.at[x, ahead], to_xr)
        send(right.at[0, rows(back)], r_buf.at[x, rows(back)], rs.at[1, step], rr.at[x, back], to_xl)
        if step < 2:
            ahead, back = lo + step, lo + 1 - step
            send(psi.at[rows(ahead)], p_buf.at[y, rows(ahead)], ps.at[0, step], pr.at[y, ahead], to_yr)
            send(psi.at[rows(back)], p_buf.at[y, rows(back)], ps.at[1, step], pr.at[y, back], to_yl)
    for step in range(4):
        ahead, back = step, (step + 2) % 4
        send(m_buf.at[y, rows(ahead)], m_buf.at[y, rows(ahead)], ms.at[0, step], mr.at[y, ahead], to_yr)
        send(m_buf.at[y, rows(back)], m_buf.at[y, rows(back)], ms.at[1, step], mr.at[y, back], to_yl)

    def take(buf, sem, block, k):
        arrived(buf.at[block, rows(k)], sem.at[block, k])

    def relay(buf, ssem, sem, block, k, device):
        take(buf, sem, block, k)
        send(buf.at[block, rows(k)], buf.at[block, rows(k)], ssem, sem.at[block, k], device)

    def share(block, k, n):
        send(p_buf.at[block, rows(k)], p_buf.at[block, rows(k)], fs.at[n], pr.at[block, k], twin)

    relay(p_buf, ps.at[0, 2], pr, yl, lo, to_yr)
    share(yl, lo, 0)
    relay(p_buf, ps.at[1, 2], pr, yr, lo + 1, to_yl)
    share(yr, lo + 1, 1)
    relay(r_buf, rs.at[0, 4], rr, xl, 0, to_xr)
    relay(r_buf, rs.at[1, 4], rr, xr, 2, to_xl)
    greeted(0, 1)
    greet(1, 2)
    take(p_buf, pr, yl, lo + 1)
    share(yl, lo + 1, 2)
    take(p_buf, pr, yr, lo)
    share(yr, lo, 3)
    relay(r_buf, rs.at[0, 5], rr, xl, 1, to_xr)
    relay(r_buf, rs.at[1, 5], rr, xr, 3, to_xl)
    greeted(1, 2)
    greet(2, 4)
    take(p_buf, pr, yo, lo)
    share(yo, lo, 4)
    take(p_buf, pr, yo, lo + 1)
    share(yo, lo + 1, 5)
    for block in (yl, yr, yo):
        for k in range(2):
            take(p_buf, pr, block, 2 - lo + k)
    load_p.wait()
    load_r.wait()

    def products(block):
        for half in range(2):
            value = dot_nt(r_buf[block], p_buf[2 * half : 2 * half + 2].reshape(2 * B, W))
            q_buf[block, x, :, 2 * half * B : 2 * (half + 1) * B] = value.astype(BF16)

    products(x)
    greeted(2, 4)
    greet(3, 8)
    take(r_buf, rr, xl, 2)
    take(r_buf, rr, xl, 3)
    products(xl)
    relay(m_buf, ms.at[0, 4], mr, yl, 0, to_yr)
    relay(m_buf, ms.at[1, 4], mr, yr, 2, to_yl)
    take(r_buf, rr, xr, 0)
    take(r_buf, rr, xr, 1)
    products(xr)
    relay(m_buf, ms.at[0, 5], mr, yl, 1, to_yr)
    relay(m_buf, ms.at[1, 5], mr, yr, 3, to_yl)
    for k in (0, 2, 1, 3):
        take(r_buf, rr, xo, k)
    products(xo)

    near = ((y - z) % N + NZ + 1) % N - 1
    first = ((z + near + NZ) % NZ) // N
    order = [(first + k) % N for k in (2, 1, 3, 0)]

    def spread(u):
        ab = order[u]
        send(q_buf.at[ab, x], q_buf.at[ab, x], qs.at[0, u], qr.at[ab, x, 0], to_xr)
        send(q_buf.at[ab, x], q_buf.at[ab, x], qs.at[1, u], qr.at[ab, x, 0], to_xl)

    def pass_on(u):
        ab = order[u]
        arrived(q_buf.at[ab, xl], qr.at[ab, xl, 0])
        part = q_buf.at[ab, xl, pl.ds(0, B // 2)]
        send(part, part, qs.at[2, u], qr.at[ab, xl, 0], to_xr)
        arrived(q_buf.at[ab, xr], qr.at[ab, xr, 0])
        part = q_buf.at[ab, xr, pl.ds(B // 2, B // 2)]
        send(part, part, qs.at[3, u], qr.at[ab, xr, 1], to_xl)

    def last_part(u):
        ab = order[u]
        arrived(q_buf.at[ab, xo, pl.ds(0, B // 2)], qr.at[ab, xo, 0])
        arrived(q_buf.at[ab, xo, pl.ds(B // 2, B // 2)], qr.at[ab, xo, 1])

    def terms(u, blocks, add):
        ab = order[u]
        for half in range(2):
            total = s_buf[u, half] if add else None
            for xk in blocks:
                cols = pl.ds(pl.multiple_of(xk * N * B, N * B), N * B)
                rhs = m_buf[2 * half : 2 * half + 2, :, cols].reshape(2 * B, N * B)
                value = dot_nt(q_buf[ab, xk], rhs)
                total = value if total is None else total + value
            s_buf[u, half] = total

    def exchange(u):
        send(s_buf.at[u, 1 - c], e_buf.at[u], es.at[u], er.at[u], twin)

    homes = []

    def home(u):
        arrived(e_buf.at[u], er.at[u])
        total = (s_buf[u, c] + e_buf[u]).astype(BF16)
        z2 = order[u] * N + y
        for j in range(2):
            t_buf[u, j] = total[:, j * B : (j + 1) * B]
        for c2 in range(2):
            for j in range(2):
                y2 = 2 * c + j
                mine = (z2 == z) & (c == c2) & (y == y2)
                src = t_buf.at[u, j, pl.ds(c2 * B // 2, B // 2)]
                local = pltpu.make_async_copy(src, g_buf.at[z], zr)
                away = pltpu.make_async_remote_copy(
                    src_ref=src, dst_ref=g_buf.at[z], send_sem=zs.at[u, 2 * c2 + j], recv_sem=zr,
                    device_id=(z2 * 2 + c2, x * N + y2), device_id_type=MESH,
                )
                pl.when(mine)(local.start)
                pl.when(jnp.logical_not(mine))(away.start)
                homes.append((mine, away))

    spread(0)
    spread(1)
    for block, ks in ((yl, (2, 3)), (yr, (0, 1))):
        for k in ks:
            take(m_buf, mr, block, k)
    pass_on(0)
    spread(2)
    for k in (0, 2, 1, 3):
        take(m_buf, mr, yo, k)
    pass_on(1)
    spread(3)
    last_part(0)
    terms(0, (0, 1, 2, 3), False)
    exchange(0)
    greeted(3, 8)
    pass_on(2)
    home(0)
    last_part(1)
    terms(1, (0, 1, 2, 3), False)
    exchange(1)
    pass_on(3)
    home(1)
    last_part(2)
    terms(2, (0, 1, 2, 3), False)
    exchange(2)
    terms(3, (x, xl, xr), False)
    home(2)
    last_part(3)
    terms(3, (xo,), True)
    exchange(3)
    home(3)

    pltpu.make_async_copy(g_buf, g_buf, zr).wait()
    total = g_buf[0].astype(F32)
    for k in range(1, NZ):
        total = total + g_buf[k].astype(F32)
    out[...] = jnp.transpose(total).astype(BF16)

    for copy in sent:
        copy.wait_send()
    for mine, away in homes:
        pl.when(jnp.logical_not(mine))(away.wait_send)


def shards(psi, left, right, mask):
    dma = pltpu.SemaphoreType.DMA
    anywhere = pl.BlockSpec(memory_space=pl.ANY)
    return pl.pallas_call(
        kernel,
        out_shape=jax.ShapeDtypeStruct((B, B // 2), BF16),
        in_specs=[anywhere, anywhere, anywhere, pl.BlockSpec(memory_space=pltpu.SMEM)],
        out_specs=pl.BlockSpec(memory_space=pltpu.VMEM),
        scratch_shapes=[
            pltpu.VMEM((N, B, W), BF16),
            pltpu.VMEM((N, B, W), BF16),
            pltpu.VMEM((N, B, W), BF16),
            pltpu.VMEM((B, W), BF16),
            pltpu.VMEM((N, N, B, N * B), BF16),
            pltpu.VMEM((N, 2, B, 2 * B), F32),
            pltpu.VMEM((N, B, 2 * B), F32),
            pltpu.VMEM((N, 2, B, B), BF16),
            pltpu.VMEM((NZ, B // 2, B), BF16),
            dma((3,)),
            dma((2, 6)), dma((N, 4)),
            dma((2, 3)), dma((N, 4)), dma((6,)),
            dma((2, 6)), dma((N, 4)),
            dma((4, N)), dma((N, N, 2)),
            dma((N,)), dma((N,)),
            dma((N, 4)), dma,
            pltpu.SemaphoreType.REGULAR((4, 2)),
        ],
        compiler_params=pltpu.CompilerParams(
            collective_id=0, has_side_effects=True, vmem_limit_bytes=60 << 20
        ),
    )(psi, left, right, mask)


def solution(mesh):
    in_specs = (P("row", None), P("term", "row", None), P("term", "row", None), P("term", "row", None))
    return jax.shard_map(
        shards, mesh=mesh, in_specs=in_specs, out_specs=P("row", "term"), check_vma=False
    )
```

time: 254 us -> 78.1 us (0.31)
  waiting for transfers between devices: 144 us -> 0 us
  Pallas kernels: 0 us -> 76.4 us
  blocking collectives: 68.6 us -> 0 us
  between operations: 13.5 us -> 0.01 us
  starting transfers between devices: 11.1 us -> 0 us
  matrix products: 9.58 us -> 0 us
  other arithmetic: 3.29 us -> 0 us
    all_gather x2 -> x0, waiting for transfers between devices: 143 us -> none  [the longest x1 84.8 us: shards(): lax.all_gather(both_right, 'row', axis=1, tiled=True)]
    pallas_call x0 -> x1, Pallas kernels: none -> 76.4 us  [shards(): pl.pallas_call(kernel, out_shape=jax.ShapeDtypeStruct((B, B // 2), BF16),...]
    all_to_all x1 -> x0, blocking collectives: 68.6 us -> none  [summed_on_arrival(): parts = lax.all_to_all(split_up(array, dim, size), axis, 0, 0, tiled=True)]
    ppermute x2 -> x0, starting transfers between devices: 11 us -> none  [swapped(): return lax.ppermute(value, axis, pairs)]
    dot_general x3 -> x0, matrix products: 9.58 us -> none  [the longest x1 5.78 us: shards(): jnp.einsum('kih,kah->ia', inner, lax.all_gather(both_right, 'row', axis=1...]
  transfers between devices with their start and end apart: 4 -> 0, of which waited for: 3 -> 0; matrix products, arithmetic and copies ran while one was open for 3% -> 0% of each run, Pallas kernels for 0% -> 0%
where the time goes in v1:
time: 78.1 us; the launch traced here: 77.9 us
  Pallas kernels  76.4 us (98%)
  local copies, waits for them, and re-layouts  1.45 us (2%)
    pallas_call x1, Pallas kernels, shards(): pl.pallas_call(kernel, out_shape=jax.ShapeDtypeStruct((B, B // 2), BF16),...  76.4 us

profile of v1, /device:TPU:1, one launch (start us, length us, event | category | flops | bytes accessed | tf_op | source)
XLA Modules:
  0.0 77.9 jit_solution(15632121929589435174)
XLA Ops:
  0.0 76.4 %shard_map.46 = bf16[128,64]{1,0:T(8,128)(2,1)} custom-call(bf16[128,2048]{1,0:T(8,128)(2,1)} %psi.1, bf16[1,128,2048]{2,1,0:T(8,128)(2,1)} %left.1, bf16[1,128,2048]{2,1,0:T(8,128)(2,1)} %right.1, s32[1,1,16]{2,1,0:T(1,128)} %mask.1), custom_call_target="tpu_custom_call" | custom-call | tf_op jit(solution)/shard_map/pallas_call | solution.py:267
  76.4 1.4 %copy.5 = bf16[128,64]{0,1:T(8,128)(2,1)} copy(bf16[128,64]{1,0:T(8,128)(2,1)} %shard_map.46) | data formatting | bytes 32768 | tf_op jit(solution)/shard_map/pallas_call | solution.py:267

commit v2 on v1

--- a/solution.py
+++ b/solution.py
@@ -11,6 +11,7 @@
 B = 128
 CH = 32
 W = 2048
+ORDER = ((1, 2, 3, 0), (0, 2, 3, 1), (0, 1, 3, 2), (1, 0, 2, 3))
 F32 = jnp.float32
 BF16 = jnp.bfloat16
 
@@ -22,7 +23,7 @@
 def kernel(
     psi, left, right, mask, out,
     p_buf, r_buf, m_buf, l_buf, q_buf, s_buf, e_buf, t_buf, g_buf,
-    load_sem, rs, rr, ps, pr, fs, ms, mr, qs, qr, es, er, zs, zr, hs,
+    load_sem, rs, rr, ps, pr, fs, ms, mr, qs, qr, es, er, zs, zr, hs, gs,
 ):
     t = lax.axis_index("term")
     row = lax.axis_index("row")
@@ -59,9 +60,7 @@
     load_r.start()
 
     barrier = pltpu.get_barrier_semaphore()
-    peers = [to_xl, to_xr, twin, along_z(1), along_z(-1)]
-    for other in (yl, yr, yo):
-        peers += [(t, x * N + other), (z * 2 + 1 - c, x * N + other)]
+    peers = [to_xl, to_xr, to_yl, to_yr, twin, along_z(1), along_z(-1)]
     for peer in peers:
         pl.semaphore_signal(barrier, inc=1, device_id=peer, device_id_type=MESH)
 
@@ -85,47 +84,51 @@
     def rows(k):
         return pl.ds(k * CH, CH)
 
-    greet(0, 1)
     lo = 2 * c
     for step in range(4):
         ahead, back = step, (step + 2) % 4
+        if step < 2:
+            send(psi.at[rows(lo + step)], p_buf.at[y, rows(lo + step)], ps.at[0, step], pr.at[y, lo + step], to_yr)
+            other = lo + 1 - step
+            send(psi.at[rows(other)], p_buf.at[y, rows(other)], ps.at[1, step], pr.at[y, other], to_yl)
         send(right.at[0, rows(ahead)], r_buf.at[x, rows(ahead)], rs.at[0, step], rr.at[x, ahead], to_xr)
         send(right.at[0, rows(back)], r_buf.at[x, rows(back)], rs.at[1, step], rr.at[x, back], to_xl)
-        if step < 2:
-            ahead, back = lo + step, lo + 1 - step
-            send(psi.at[rows(ahead)], p_buf.at[y, rows(ahead)], ps.at[0, step], pr.at[y, ahead], to_yr)
-            send(psi.at[rows(back)], p_buf.at[y, rows(back)], ps.at[1, step], pr.at[y, back], to_yl)
+    for k, device in enumerate((to_yl, to_yr)):
+        pl.semaphore_signal(gs.at[k], inc=1, device_id=device, device_id_type=MESH)
+
+    def take(buf, sem, block, k):
+        arrived(buf.at[block, rows(k)], sem.at[block, k])
+
+    def relay(buf, ssem, sem, block, k, device):
+        take(buf, sem, block, k)
+        send(buf.at[block, rows(k)], buf.at[block, rows(k)], ssem, sem.at[block, k], device)
+
+    def share(block, k, n):
+        send(p_buf.at[block, rows(k)], p_buf.at[block, rows(k)], fs.at[n], pr.at[block, k], twin)
+
+    relay(p_buf, ps.at[0, 2], pr, yl, lo, to_yr)
+    relay(p_buf, ps.at[1, 2], pr, yr, lo + 1, to_yl)
     for step in range(4):
         ahead, back = step, (step + 2) % 4
         send(m_buf.at[y, rows(ahead)], m_buf.at[y, rows(ahead)], ms.at[0, step], mr.at[y, ahead], to_yr)
         send(m_buf.at[y, rows(back)], m_buf.at[y, rows(back)], ms.at[1, step], mr.at[y, back], to_yl)
-
-    def take(buf, sem, block, k):
-        arrived(buf.at[block, rows(k)], sem.at[block, k])
-
-    def relay(buf, ssem, sem, block, k, device):
-        take(buf, sem, block, k)
-        send(buf.at[block, rows(k)], buf.at[block, rows(k)], ssem, sem.at[block, k], device)
-
-    def share(block, k, n):
-        send(p_buf.at[block, rows(k)], p_buf.at[block, rows(k)], fs.at[n], pr.at[block, k], twin)
-
-    relay(p_buf, ps.at[0, 2], pr, yl, lo, to_yr)
     share(yl, lo, 0)
-    relay(p_buf, ps.at[1, 2], pr, yr, lo + 1, to_yl)
     share(yr, lo + 1, 1)
     relay(r_buf, rs.at[0, 4], rr, xl, 0, to_xr)
     relay(r_buf, rs.at[1, 4], rr, xr, 2, to_xl)
-    greeted(0, 1)
-    greet(1, 2)
+    pl.semaphore_wait(gs.at[0], 1)
+    pl.semaphore_wait(gs.at[1], 1)
+    pl.semaphore_signal(gs.at[2], inc=1, device_id=twin, device_id_type=MESH)
+    pl.semaphore_wait(gs.at[2], 1)
+    greet(0, 1)
     take(p_buf, pr, yl, lo + 1)
     share(yl, lo + 1, 2)
     take(p_buf, pr, yr, lo)
     share(yr, lo, 3)
     relay(r_buf, rs.at[0, 5], rr, xl, 1, to_xr)
     relay(r_buf, rs.at[1, 5], rr, xr, 3, to_xl)
-    greeted(1, 2)
-    greet(2, 4)
+    greeted(0, 1)
+    greet(1, 2)
     take(p_buf, pr, yo, lo)
     share(yo, lo, 4)
     take(p_buf, pr, yo, lo + 1)
@@ -135,35 +138,33 @@
             take(p_buf, pr, block, 2 - lo + k)
     load_p.wait()
     load_r.wait()
+    greeted(1, 2)
+    greet(2, 4)
 
     def products(block):
         for half in range(2):
             value = dot_nt(r_buf[block], p_buf[2 * half : 2 * half + 2].reshape(2 * B, W))
             q_buf[block, x, :, 2 * half * B : 2 * (half + 1) * B] = value.astype(BF16)
 
+    group = z // N
+    order = [sum((group == k).astype(jnp.int32) * ORDER[k][u] for k in range(N)) for u in range(N)]
+    swap = (order[0] == xo).astype(jnp.int32)
+    sends = [order[0] + swap * (order[1] - order[0]), order[1] + swap * (order[0] - order[1]), order[2], order[3]]
+
     products(x)
-    greeted(2, 4)
-    greet(3, 8)
     take(r_buf, rr, xl, 2)
     take(r_buf, rr, xl, 3)
     products(xl)
-    relay(m_buf, ms.at[0, 4], mr, yl, 0, to_yr)
-    relay(m_buf, ms.at[1, 4], mr, yr, 2, to_yl)
     take(r_buf, rr, xr, 0)
     take(r_buf, rr, xr, 1)
     products(xr)
-    relay(m_buf, ms.at[0, 5], mr, yl, 1, to_yr)
-    relay(m_buf, ms.at[1, 5], mr, yr, 3, to_yl)
-    for k in (0, 2, 1, 3):
-        take(r_buf, rr, xo, k)
-    products(xo)
-
-    near = ((y - z) % N + NZ + 1) % N - 1
-    first = ((z + near + NZ) % NZ) // N
-    order = [(first + k) % N for k in (2, 1, 3, 0)]
+    greeted(2, 4)
+    greet(3, 8)
+    relay(m_buf, ms.at[0, 4], mr, yl, 0, to_yr)
+    relay(m_buf, ms.at[1, 4], mr, yr, 2, to_yl)
 
     def spread(u):
-        ab = order[u]
+        ab = sends[u]
         send(q_buf.at[ab, x], q_buf.at[ab, x], qs.at[0, u], qr.at[ab, x, 0], to_xr)
         send(q_buf.at[ab, x], q_buf.at[ab, x], qs.at[1, u], qr.at[ab, x, 0], to_xl)
 
@@ -197,48 +198,61 @@
 
     homes = []
 
+    def deliver(src, z2, c2, y2, slot, ssem):
+        mine = (z2 == z) & (c == c2) & (y == y2)
+        local = pltpu.make_async_copy(src, g_buf.at[slot], zr)
+        away = pltpu.make_async_remote_copy(
+            src_ref=src, dst_ref=g_buf.at[slot], send_sem=ssem, recv_sem=zr,
+            device_id=(z2 * 2 + c2, x * N + y2), device_id_type=MESH,
+        )
+        pl.when(mine)(local.start)
+        pl.when(jnp.logical_not(mine))(away.start)
+        homes.append((mine, away))
+
     def home(u):
         arrived(e_buf.at[u], er.at[u])
         total = (s_buf[u, c] + e_buf[u]).astype(BF16)
-        z2 = order[u] * N + y
         for j in range(2):
             t_buf[u, j] = total[:, j * B : (j + 1) * B]
         for c2 in range(2):
             for j in range(2):
-                y2 = 2 * c + j
-                mine = (z2 == z) & (c == c2) & (y == y2)
                 src = t_buf.at[u, j, pl.ds(c2 * B // 2, B // 2)]
-                local = pltpu.make_async_copy(src, g_buf.at[z], zr)
-                away = pltpu.make_async_remote_copy(
-                    src_ref=src, dst_ref=g_buf.at[z], send_sem=zs.at[u, 2 * c2 + j], recv_sem=zr,
-                    device_id=(z2 * 2 + c2, x * N + y2), device_id_type=MESH,
-                )
-                pl.when(mine)(local.start)
-                pl.when(jnp.logical_not(mine))(away.start)
-                homes.append((mine, away))
+                deliver(src, order[u] * N + y, c2, 2 * c + j, z, zs.at[u, 2 * c2 + j])
+
+    def home_apart():
+        for y2 in range(N):
+            for c2 in range(2):
+                src = t_buf.at[3 + y2 // 2, y2 % 2, pl.ds(c2 * B // 2, B // 2)]
+                slot = jnp.where(c == y2 // 2, z, NZ + z % N)
+                deliver(src, group * N + y, c2, y2, slot, zs.at[3 + y2 // 2, 2 * c2 + y2 % 2])
 
     spread(0)
+    relay(m_buf, ms.at[0, 5], mr, yl, 1, to_yr)
+    relay(m_buf, ms.at[1, 5], mr, yr, 3, to_yl)
+    for k in (0, 2, 1, 3):
+        take(r_buf, rr, xo, k)
+    products(xo)
     spread(1)
     for block, ks in ((yl, (2, 3)), (yr, (0, 1))):
         for k in ks:
             take(m_buf, mr, block, k)
     pass_on(0)
     spread(2)
+    pass_on(1)
+    spread(3)
     for k in (0, 2, 1, 3):
         take(m_buf, mr, yo, k)
-    pass_on(1)
-    spread(3)
     last_part(0)
     terms(0, (0, 1, 2, 3), False)
     exchange(0)
     greeted(3, 8)
+    home(0)
     pass_on(2)
-    home(0)
     last_part(1)
     terms(1, (0, 1, 2, 3), False)
     exchange(1)
+    home(1)
     pass_on(3)
-    home(1)
     last_part(2)
     terms(2, (0, 1, 2, 3), False)
     exchange(2)
@@ -246,14 +260,16 @@
     home(2)
     last_part(3)
     terms(3, (xo,), True)
-    exchange(3)
-    home(3)
+    for half in range(2):
+        for j in range(2):
+            t_buf[3 + half, j] = s_buf[3, half, :, j * B : (j + 1) * B].astype(BF16)
+    home_apart()
 
     pltpu.make_async_copy(g_buf, g_buf, zr).wait()
     total = g_buf[0].astype(F32)
-    for k in range(1, NZ):
+    for k in range(1, NZ + N):
         total = total + g_buf[k].astype(F32)
-    out[...] = jnp.transpose(total).astype(BF16)
+    out[...] = total.astype(BF16)
 
     for copy in sent:
         copy.wait_send()
@@ -266,7 +282,7 @@
     anywhere = pl.BlockSpec(memory_space=pl.ANY)
     return pl.pallas_call(
         kernel,
-        out_shape=jax.ShapeDtypeStruct((B, B // 2), BF16),
+        out_shape=jax.ShapeDtypeStruct((B // 2, B), BF16),
         in_specs=[anywhere, anywhere, anywhere, pl.BlockSpec(memory_space=pltpu.SMEM)],
         out_specs=pl.BlockSpec(memory_space=pltpu.VMEM),
         scratch_shapes=[
@@ -276,22 +292,22 @@
             pltpu.VMEM((B, W), BF16),
             pltpu.VMEM((N, N, B, N * B), BF16),
             pltpu.VMEM((N, 2, B, 2 * B), F32),
-            pltpu.VMEM((N, B, 2 * B), F32),
-            pltpu.VMEM((N, 2, B, B), BF16),
-            pltpu.VMEM((NZ, B // 2, B), BF16),
+            pltpu.VMEM((N - 1, B, 2 * B), F32),
+            pltpu.VMEM((N + 1, 2, B, B), BF16),
+            pltpu.VMEM((NZ + N, B // 2, B), BF16),
             dma((3,)),
             dma((2, 6)), dma((N, 4)),
             dma((2, 3)), dma((N, 4)), dma((6,)),
             dma((2, 6)), dma((N, 4)),
             dma((4, N)), dma((N, N, 2)),
-            dma((N,)), dma((N,)),
-            dma((N, 4)), dma,
-            pltpu.SemaphoreType.REGULAR((4, 2)),
+            dma((N - 1,)), dma((N - 1,)),
+            dma((N + 1, 4)), dma,
+            pltpu.SemaphoreType.REGULAR((4, 2)), pltpu.SemaphoreType.REGULAR((3,)),
         ],
         compiler_params=pltpu.CompilerParams(
             collective_id=0, has_side_effects=True, vmem_limit_bytes=60 << 20
         ),
-    )(psi, left, right, mask)
+    )(psi, left, right, mask).T
 
 
 def solution(mesh):

time: 78.1 us -> 68.1 us (0.87)
  the two profiles are of different devices: /device:TPU:1 before, /device:TPU:27 now
where the time goes in v2:
time: 68.1 us; the launch traced here: 67.9 us
  Pallas kernels  66.5 us (98%)
  local copies, waits for them, and re-layouts  1.32 us (2%)
    pallas_call x1, Pallas kernels, shards(): pl.pallas_call(kernel, out_shape=jax.ShapeDtypeStruct((B // 2, B), BF16),...  66.5 us

profile of v2, /device:TPU:27, one launch (start us, length us, event | category | flops | bytes accessed | tf_op | source)
XLA Modules:
  0.0 67.9 jit_solution(9384188112531324310)
XLA Ops:
  0.0 66.5 %shard_map.46 = bf16[64,128]{1,0:T(8,128)(2,1)} custom-call(bf16[128,2048]{1,0:T(8,128)(2,1)} %psi.1, bf16[1,128,2048]{2,1,0:T(8,128)(2,1)} %left.1, bf16[1,128,2048]{2,1,0:T(8,128)(2,1)} %right.1, s32[1,1,16]{2,1,0:T(1,128)} %mask.1), custom_call_target="tpu_custom_call" | custom-call | tf_op jit(solution)/shard_map/pallas_call | solution.py:283
  66.5 1.3 %copy.6 = bf16[128,64]{0,1:T(8,128)(2,1)} copy(bf16[128,64]{0,1:T(8,128)(2,1)} %bitcast.1) | data formatting | bytes 32768

commit v3 on v2

--- a/solution.py
+++ b/solution.py
@@ -8,10 +8,11 @@
 MESH = pl.DeviceIdType.MESH
 N = 4
 NZ = 16
+G = N - 1 + N
 B = 128
 CH = 32
 W = 2048
-ORDER = ((1, 2, 3, 0), (0, 2, 3, 1), (0, 1, 3, 2), (1, 0, 2, 3))
+ORDER = ((1, 2, 3, 0), (0, 2, 3, 1), (0, 1, 3, 2), (0, 1, 2, 3))
 F32 = jnp.float32
 BF16 = jnp.bfloat16
 
@@ -22,8 +23,8 @@
 
 def kernel(
     psi, left, right, mask, out,
-    p_buf, r_buf, m_buf, l_buf, q_buf, s_buf, e_buf, t_buf, g_buf,
-    load_sem, rs, rr, ps, pr, fs, ms, mr, qs, qr, es, er, zs, zr, hs, gs,
+    p_buf, r_buf, m_buf, l_buf, q_buf, s_buf, e_buf, t_buf, g_buf, l1_buf, f_buf,
+    load_sem, rs, rr, ps, pr, fs, ms, mr, qs, qr, es, er, zs, zr, l1s, l1r, hs, gs,
 ):
     t = lax.axis_index("term")
     row = lax.axis_index("row")
@@ -197,6 +198,8 @@
         send(s_buf.at[u, 1 - c], e_buf.at[u], es.at[u], er.at[u], twin)
 
     homes = []
+    place = z % N
+    collector = c == place // 2
 
     def deliver(src, z2, c2, y2, slot, ssem):
         mine = (z2 == z) & (c == c2) & (y == y2)
@@ -207,24 +210,57 @@
         )
         pl.when(mine)(local.start)
         pl.when(jnp.logical_not(mine))(away.start)
-        homes.append((mine, away))
-
-    def home(u):
+        homes.append((jnp.logical_not(mine), away))
+
+    def gather(u):
         arrived(e_buf.at[u], er.at[u])
-        total = (s_buf[u, c] + e_buf[u]).astype(BF16)
-        for j in range(2):
-            t_buf[u, j] = total[:, j * B : (j + 1) * B]
-        for c2 in range(2):
-            for j in range(2):
-                src = t_buf.at[u, j, pl.ds(c2 * B // 2, B // 2)]
-                deliver(src, order[u] * N + y, c2, 2 * c + j, z, zs.at[u, 2 * c2 + j])
-
-    def home_apart():
-        for y2 in range(N):
+        s_buf[u, c] = s_buf[u, c] + e_buf[u]
+        for k in range(2):
+            t_buf[u, k] = s_buf[u, c, :, k * B : (k + 1) * B].astype(BF16)
+            there = 2 * c + k
+            away = pltpu.make_async_remote_copy(
+                src_ref=t_buf.at[u, k], dst_ref=l1_buf.at[u, place], send_sem=l1s.at[u, k], recv_sem=l1r.at[u, place],
+                device_id=((group * N + there) * 2 + c, row), device_id_type=MESH,
+            )
+            other = there != place
+            pl.when(other)(away.start)
+            homes.append((other, away))
+
+    def collect(u):
+        @pl.when(collector)
+        def _():
+            total = s_buf[u, c, :, pl.ds(pl.multiple_of((place % 2) * B, B), B)]
+            for k in range(1, N):
+                source = (place + k) % N
+                arrived(l1_buf.at[u, source], l1r.at[u, source])
+                total = total + l1_buf[u, source].astype(F32)
+            f_buf[u] = total.astype(BF16)
+            slot = (group - order[u] + N) % N - 1
             for c2 in range(2):
-                src = t_buf.at[3 + y2 // 2, y2 % 2, pl.ds(c2 * B // 2, B // 2)]
-                slot = jnp.where(c == y2 // 2, z, NZ + z % N)
-                deliver(src, group * N + y, c2, y2, slot, zs.at[3 + y2 // 2, 2 * c2 + y2 % 2])
+                pltpu.make_async_remote_copy(
+                    src_ref=f_buf.at[u, pl.ds(c2 * B // 2, B // 2)], dst_ref=g_buf.at[slot],
+                    send_sem=zs.at[u, c2], recv_sem=zr,
+                    device_id=((order[u] * N + y) * 2 + c2, x * N + place), device_id_type=MESH,
+                ).start()
+
+    def collected(u):
+        @pl.when(collector)
+        def _():
+            for c2 in range(2):
+                pltpu.make_async_remote_copy(
+                    src_ref=f_buf.at[u, pl.ds(c2 * B // 2, B // 2)], dst_ref=g_buf.at[0],
+                    send_sem=zs.at[u, c2], recv_sem=zr, device_id=twin, device_id_type=MESH,
+                ).wait_send()
+
+    def home_own():
+        arrived(e_buf.at[3], er.at[3])
+        total = (s_buf[3, c] + e_buf[3]).astype(BF16)
+        for k in range(2):
+            t_buf[3, k] = total[:, k * B : (k + 1) * B]
+        for k in range(2):
+            for c2 in range(2):
+                src = t_buf.at[3, k, pl.ds(c2 * B // 2, B // 2)]
+                deliver(src, group * N + y, c2, 2 * c + k, 3 + place, zs.at[3, 2 * c2 + k])
 
     spread(0)
     relay(m_buf, ms.at[0, 5], mr, yl, 1, to_yr)
@@ -246,35 +282,38 @@
     terms(0, (0, 1, 2, 3), False)
     exchange(0)
     greeted(3, 8)
-    home(0)
+    gather(0)
     pass_on(2)
     last_part(1)
     terms(1, (0, 1, 2, 3), False)
     exchange(1)
-    home(1)
+    collect(0)
+    gather(1)
     pass_on(3)
     last_part(2)
     terms(2, (0, 1, 2, 3), False)
     exchange(2)
     terms(3, (x, xl, xr), False)
-    home(2)
+    gather(2)
+    collect(1)
     last_part(3)
     terms(3, (xo,), True)
-    for half in range(2):
-        for j in range(2):
-            t_buf[3 + half, j] = s_buf[3, half, :, j * B : (j + 1) * B].astype(BF16)
-    home_apart()
+    exchange(3)
+    collect(2)
+    home_own()
 
     pltpu.make_async_copy(g_buf, g_buf, zr).wait()
     total = g_buf[0].astype(F32)
-    for k in range(1, NZ + N):
+    for k in range(1, G):
         total = total + g_buf[k].astype(F32)
     out[...] = total.astype(BF16)
 
     for copy in sent:
         copy.wait_send()
-    for mine, away in homes:
-        pl.when(jnp.logical_not(mine))(away.wait_send)
+    for started, away in homes:
+        pl.when(started)(away.wait_send)
+    for u in range(N - 1):
+        collected(u)
 
 
 def shards(psi, left, right, mask):
@@ -292,16 +331,18 @@
             pltpu.VMEM((B, W), BF16),
             pltpu.VMEM((N, N, B, N * B), BF16),
             pltpu.VMEM((N, 2, B, 2 * B), F32),
-            pltpu.VMEM((N - 1, B, 2 * B), F32),
-            pltpu.VMEM((N + 1, 2, B, B), BF16),
-            pltpu.VMEM((NZ + N, B // 2, B), BF16),
+            pltpu.VMEM((N, B, 2 * B), F32),
+            pltpu.VMEM((N, 2, B, B), BF16),
+            pltpu.VMEM((G, B // 2, B), BF16),
+            pltpu.VMEM((N - 1, N, B, B), BF16),
+            pltpu.VMEM((N - 1, B, B), BF16),
             dma((3,)),
             dma((2, 6)), dma((N, 4)),
             dma((2, 3)), dma((N, 4)), dma((6,)),
             dma((2, 6)), dma((N, 4)),
             dma((4, N)), dma((N, N, 2)),
-            dma((N - 1,)), dma((N - 1,)),
-            dma((N + 1, 4)), dma,
+            dma((N,)), dma((N,)),
+            dma((N, 4)), dma, dma((N - 1, 2)), dma((N - 1, N)),
             pltpu.SemaphoreType.REGULAR((4, 2)), pltpu.SemaphoreType.REGULAR((3,)),
         ],
         compiler_params=pltpu.CompilerParams(

time: 68.1 us -> 64.7 us (0.950)
  the two profiles are of different devices: /device:TPU:27 before, /device:TPU:1 now
where the time goes in v3:
time: 64.7 us; the launch traced here: 64.4 us
  Pallas kernels  63.1 us (98%)
  local copies, waits for them, and re-layouts  1.32 us (2%)
    pallas_call x1, Pallas kernels, shards(): pl.pallas_call(kernel, out_shape=jax.ShapeDtypeStruct((B // 2, B), BF16),...  63.1 us
    unnamed x1, local copies, waits for them, and re-layouts  1.32 us

profile of v3, /device:TPU:1, one launch (start us, length us, event | category | flops | bytes accessed | tf_op | source)
XLA Modules:
  0.0 64.4 jit_solution(8280897388782671182)
XLA Ops:
  0.0 63.1 %shard_map.46 = bf16[64,128]{1,0:T(8,128)(2,1)} custom-call(bf16[128,2048]{1,0:T(8,128)(2,1)} %psi.1, bf16[1,128,2048]{2,1,0:T(8,128)(2,1)} %left.1, bf16[1,128,2048]{2,1,0:T(8,128)(2,1)} %right.1, s32[1,1,16]{2,1,0:T(1,128)} %mask.1), custom_call_target="tpu_custom_call" | custom-call | tf_op jit(solution)/shard_map/pallas_call | solution.py:322
  63.1 1.3 %copy.6 = bf16[128,64]{0,1:T(8,128)(2,1)} copy(bf16[128,64]{0,1:T(8,128)(2,1)} %bitcast.1) | data formatting | bytes 32768

commit v4 on v3

--- a/solution.py
+++ b/solution.py
@@ -12,7 +12,7 @@
 B = 128
 CH = 32
 W = 2048
-ORDER = ((1, 2, 3, 0), (0, 2, 3, 1), (0, 1, 3, 2), (0, 1, 2, 3))
+ORDER = ((0, 1, 2, 3), (0, 2, 3, 1), (0, 1, 3, 2), (0, 1, 2, 3))
 F32 = jnp.float32
 BF16 = jnp.bfloat16
 
@@ -24,7 +24,7 @@
 def kernel(
     psi, left, right, mask, out,
     p_buf, r_buf, m_buf, l_buf, q_buf, s_buf, e_buf, t_buf, g_buf, l1_buf, f_buf,
-    load_sem, rs, rr, ps, pr, fs, ms, mr, qs, qr, es, er, zs, zr, l1s, l1r, hs, gs,
+    load_sem, rs, rr, ps, pr, fs, ms, mr, qs, qr, es, er, zs, zr, fz, l1s, l1r, hs, gs,
 ):
     t = lax.axis_index("term")
     row = lax.axis_index("row")
@@ -121,15 +121,13 @@
     pl.semaphore_wait(gs.at[1], 1)
     pl.semaphore_signal(gs.at[2], inc=1, device_id=twin, device_id_type=MESH)
     pl.semaphore_wait(gs.at[2], 1)
-    greet(0, 1)
     take(p_buf, pr, yl, lo + 1)
     share(yl, lo + 1, 2)
     take(p_buf, pr, yr, lo)
     share(yr, lo, 3)
     relay(r_buf, rs.at[0, 5], rr, xl, 1, to_xr)
     relay(r_buf, rs.at[1, 5], rr, xr, 3, to_xl)
-    greeted(0, 1)
-    greet(1, 2)
+    greet(0, 1)
     take(p_buf, pr, yo, lo)
     share(yo, lo, 4)
     take(p_buf, pr, yo, lo + 1)
@@ -139,8 +137,8 @@
             take(p_buf, pr, block, 2 - lo + k)
     load_p.wait()
     load_r.wait()
-    greeted(1, 2)
-    greet(2, 4)
+    greeted(0, 1)
+    greet(1, 2)
 
     def products(block):
         for half in range(2):
@@ -159,8 +157,8 @@
     take(r_buf, rr, xr, 0)
     take(r_buf, rr, xr, 1)
     products(xr)
-    greeted(2, 4)
-    greet(3, 8)
+    greeted(1, 2)
+    greet(2, 4)
     relay(m_buf, ms.at[0, 4], mr, yl, 0, to_yr)
     relay(m_buf, ms.at[1, 4], mr, yr, 2, to_yl)
 
@@ -201,16 +199,11 @@
     place = z % N
     collector = c == place // 2
 
-    def deliver(src, z2, c2, y2, slot, ssem):
-        mine = (z2 == z) & (c == c2) & (y == y2)
-        local = pltpu.make_async_copy(src, g_buf.at[slot], zr)
-        away = pltpu.make_async_remote_copy(
-            src_ref=src, dst_ref=g_buf.at[slot], send_sem=ssem, recv_sem=zr,
-            device_id=(z2 * 2 + c2, x * N + y2), device_id_type=MESH,
-        )
-        pl.when(mine)(local.start)
-        pl.when(jnp.logical_not(mine))(away.start)
-        homes.append((jnp.logical_not(mine), away))
+    own = [ab == group for ab in order]
+
+    def start_if(condition, copy):
+        pl.when(condition)(copy.start)
+        homes.append((condition, copy))
 
     def gather(u):
         arrived(e_buf.at[u], er.at[u])
@@ -222,12 +215,25 @@
                 src_ref=t_buf.at[u, k], dst_ref=l1_buf.at[u, place], send_sem=l1s.at[u, k], recv_sem=l1r.at[u, place],
                 device_id=((group * N + there) * 2 + c, row), device_id_type=MESH,
             )
-            other = there != place
-            pl.when(other)(away.start)
-            homes.append((other, away))
+            start_if(jnp.logical_not(own[u]) & (there != place), away)
+        for k in range(2):
+            for c2 in range(2):
+                src = t_buf.at[u, k, pl.ds(c2 * B // 2, B // 2)]
+                z2, y2, dst = group * N + y, 2 * c + k, g_buf.at[3 + place]
+                mine = (z2 == z) & (c == c2) & (y == y2)
+                local = pltpu.make_async_copy(src, dst, zr)
+                away = pltpu.make_async_remote_copy(
+                    src_ref=src, dst_ref=dst, send_sem=zs.at[u, 2 * c2 + k], recv_sem=zr,
+                    device_id=(z2 * 2 + c2, x * N + y2), device_id_type=MESH,
+                )
+                pl.when(own[u] & mine)(local.start)
+                start_if(own[u] & jnp.logical_not(mine), away)
+
+    def from_group(u):
+        return collector & jnp.logical_not(own[u])
 
     def collect(u):
-        @pl.when(collector)
+        @pl.when(from_group(u))
         def _():
             total = s_buf[u, c, :, pl.ds(pl.multiple_of((place % 2) * B, B), B)]
             for k in range(1, N):
@@ -239,28 +245,18 @@
             for c2 in range(2):
                 pltpu.make_async_remote_copy(
                     src_ref=f_buf.at[u, pl.ds(c2 * B // 2, B // 2)], dst_ref=g_buf.at[slot],
-                    send_sem=zs.at[u, c2], recv_sem=zr,
+                    send_sem=fz.at[u, c2], recv_sem=zr,
                     device_id=((order[u] * N + y) * 2 + c2, x * N + place), device_id_type=MESH,
                 ).start()
 
     def collected(u):
-        @pl.when(collector)
+        @pl.when(from_group(u))
         def _():
             for c2 in range(2):
                 pltpu.make_async_remote_copy(
                     src_ref=f_buf.at[u, pl.ds(c2 * B // 2, B // 2)], dst_ref=g_buf.at[0],
-                    send_sem=zs.at[u, c2], recv_sem=zr, device_id=twin, device_id_type=MESH,
+                    send_sem=fz.at[u, c2], recv_sem=zr, device_id=twin, device_id_type=MESH,
                 ).wait_send()
-
-    def home_own():
-        arrived(e_buf.at[3], er.at[3])
-        total = (s_buf[3, c] + e_buf[3]).astype(BF16)
-        for k in range(2):
-            t_buf[3, k] = total[:, k * B : (k + 1) * B]
-        for k in range(2):
-            for c2 in range(2):
-                src = t_buf.at[3, k, pl.ds(c2 * B // 2, B // 2)]
-                deliver(src, group * N + y, c2, 2 * c + k, 3 + place, zs.at[3, 2 * c2 + k])
 
     spread(0)
     relay(m_buf, ms.at[0, 5], mr, yl, 1, to_yr)
@@ -269,6 +265,8 @@
         take(r_buf, rr, xo, k)
     products(xo)
     spread(1)
+    greeted(2, 4)
+    greet(3, 8)
     for block, ks in ((yl, (2, 3)), (yr, (0, 1))):
         for k in ks:
             take(m_buf, mr, block, k)
@@ -281,15 +279,15 @@
     last_part(0)
     terms(0, (0, 1, 2, 3), False)
     exchange(0)
+    pass_on(2)
     greeted(3, 8)
     gather(0)
-    pass_on(2)
     last_part(1)
     terms(1, (0, 1, 2, 3), False)
     exchange(1)
-    collect(0)
     gather(1)
     pass_on(3)
+    collect(0)
     last_part(2)
     terms(2, (0, 1, 2, 3), False)
     exchange(2)
@@ -300,7 +298,8 @@
     terms(3, (xo,), True)
     exchange(3)
     collect(2)
-    home_own()
+    gather(3)
+    collect(3)
 
     pltpu.make_async_copy(g_buf, g_buf, zr).wait()
     total = g_buf[0].astype(F32)
@@ -312,7 +311,7 @@
         copy.wait_send()
     for started, away in homes:
         pl.when(started)(away.wait_send)
-    for u in range(N - 1):
+    for u in range(N):
         collected(u)
 
 
@@ -334,15 +333,15 @@
             pltpu.VMEM((N, B, 2 * B), F32),
             pltpu.VMEM((N, 2, B, B), BF16),
             pltpu.VMEM((G, B // 2, B), BF16),
-            pltpu.VMEM((N - 1, N, B, B), BF16),
-            pltpu.VMEM((N - 1, B, B), BF16),
+            pltpu.VMEM((N, N, B, B), BF16),
+            pltpu.VMEM((N, B, B), BF16),
             dma((3,)),
             dma((2, 6)), dma((N, 4)),
             dma((2, 3)), dma((N, 4)), dma((6,)),
             dma((2, 6)), dma((N, 4)),
             dma((4, N)), dma((N, N, 2)),
             dma((N,)), dma((N,)),
-            dma((N, 4)), dma, dma((N - 1, 2)), dma((N - 1, N)),
+            dma((N, 4)), dma, dma((N, 2)), dma((N, 2)), dma((N, N)),
             pltpu.SemaphoreType.REGULAR((4, 2)), pltpu.SemaphoreType.REGULAR((3,)),
         ],
         compiler_params=pltpu.CompilerParams(

time: 64.7 us -> 62.7 us (0.969)
  Pallas kernels: 63.1 us -> 60.8 us
    pallas_call x1, Pallas kernels: 63.1 us -> 60.8 us  [shards(): pl.pallas_call(kernel, out_shape=jax.ShapeDtypeStruct((B // 2, B), BF16),...]
where the time goes in v4:
time: 62.7 us; the launch traced here: 62.2 us
  Pallas kernels  60.8 us (97%)
  local copies, waits for them, and re-layouts  1.32 us (2%)
    pallas_call x1, Pallas kernels, shards(): pl.pallas_call(kernel, out_shape=jax.ShapeDtypeStruct((B // 2, B), BF16),...  60.8 us
    unnamed x1, local copies, waits for them, and re-layouts  1.32 us

profile of v4, /device:TPU:1, one launch (start us, length us, event | category | flops | bytes accessed | tf_op | source)
XLA Modules:
  0.0 62.2 jit_solution(6521630651256214469)
XLA Ops:
  0.0 60.8 %shard_map.46 = bf16[64,128]{1,0:T(8,128)(2,1)} custom-call(bf16[128,2048]{1,0:T(8,128)(2,1)} %psi.1, bf16[1,128,2048]{2,1,0:T(8,128)(2,1)} %left.1, bf16[1,128,2048]{2,1,0:T(8,128)(2,1)} %right.1, s32[1,1,16]{2,1,0:T(1,128)} %mask.1), custom_call_target="tpu_custom_call" | custom-call | tf_op jit(solution)/shard_map/pallas_call | solution.py:321
  60.9 1.3 %copy.6 = bf16[128,64]{0,1:T(8,128)(2,1)} copy(bf16[128,64]{0,1:T(8,128)(2,1)} %bitcast.1) | data formatting | bytes 32768

commit v5 on v4

--- a/solution.py
+++ b/solution.py
@@ -56,20 +56,14 @@
     load_r = pltpu.make_async_copy(right.at[0], r_buf.at[x], load_sem.at[0])
     load_p = pltpu.make_async_copy(psi, p_buf.at[y], load_sem.at[1])
     load_l = pltpu.make_async_copy(left.at[0], l_buf, load_sem.at[2])
-    load_l.start()
-    load_p.start()
-    load_r.start()
-
     barrier = pltpu.get_barrier_semaphore()
     peers = [to_xl, to_xr, to_yl, to_yr, twin, along_z(1), along_z(-1)]
     for peer in peers:
         pl.semaphore_signal(barrier, inc=1, device_id=peer, device_id_type=MESH)
 
-    load_l.wait()
-    for k in range(W // B):
-        scale = jnp.full((B, B), mask[0, 0, k].astype(F32), F32).astype(BF16)
-        m_buf[y, :, k * B : (k + 1) * B] = l_buf[:, k * B : (k + 1) * B] * scale
-
+    load_l.start()
+    load_p.start()
+    load_r.start()
     pl.semaphore_wait(barrier, len(peers))
 
     def greet(k, distance):
@@ -106,6 +100,11 @@
 
     def share(block, k, n):
         send(p_buf.at[block, rows(k)], p_buf.at[block, rows(k)], fs.at[n], pr.at[block, k], twin)
+
+    load_l.wait()
+    for k in range(W // B):
+        scale = jnp.full((B, B), mask[0, 0, k].astype(F32), F32).astype(BF16)
+        m_buf[y, :, k * B : (k + 1) * B] = l_buf[:, k * B : (k + 1) * B] * scale
 
     relay(p_buf, ps.at[0, 2], pr, yl, lo, to_yr)
     relay(p_buf, ps.at[1, 2], pr, yr, lo + 1, to_yl)
@@ -293,12 +292,12 @@
     exchange(2)
     terms(3, (x, xl, xr), False)
     gather(2)
-    collect(1)
     last_part(3)
     terms(3, (xo,), True)
     exchange(3)
+    collect(1)
+    gather(3)
     collect(2)
-    gather(3)
     collect(3)
 
     pltpu.make_async_copy(g_buf, g_buf, zr).wait()

time: 62.7 us -> 62.4 us (level)
  no operation moved by 1% of the time
where the time goes in v5:
time: 62.4 us; the launch traced here: 62.2 us
  Pallas kernels  60.9 us (98%)
  local copies, waits for them, and re-layouts  1.32 us (2%)
    pallas_call x1, Pallas kernels, shards(): pl.pallas_call(kernel, out_shape=jax.ShapeDtypeStruct((B // 2, B), BF16),...  60.9 us
    unnamed x1, local copies, waits for them, and re-layouts  1.32 us

profile of v5, /device:TPU:1, one launch (start us, length us, event | category | flops | bytes accessed | tf_op | source)
XLA Modules:
  0.0 62.2 jit_solution(13850540487959966058)
XLA Ops:
  0.0 60.9 %shard_map.46 = bf16[64,128]{1,0:T(8,128)(2,1)} custom-call(bf16[128,2048]{1,0:T(8,128)(2,1)} %psi.1, bf16[1,128,2048]{2,1,0:T(8,128)(2,1)} %left.1, bf16[1,128,2048]{2,1,0:T(8,128)(2,1)} %right.1, s32[1,1,16]{2,1,0:T(1,128)} %mask.1), custom_call_target="tpu_custom_call" | custom-call | tf_op jit(solution)/shard_map/pallas_call | solution.py:320
  60.9 1.3 %copy.6 = bf16[128,64]{0,1:T(8,128)(2,1)} copy(bf16[128,64]{0,1:T(8,128)(2,1)} %bitcast.1) | data formatting | bytes 32768

commit v6 on v5

--- a/solution.py
+++ b/solution.py
@@ -12,7 +12,7 @@
 B = 128
 CH = 32
 W = 2048
-ORDER = ((0, 1, 2, 3), (0, 2, 3, 1), (0, 1, 3, 2), (0, 1, 2, 3))
+ORDER = ((0, 1, 2, 3), (0, 3, 2, 1), (0, 1, 3, 2), (0, 1, 2, 3))
 F32 = jnp.float32
 BF16 = jnp.bfloat16
 

time: 62.4 us -> 62.4 us (level)
  no operation moved by 1% of the time
where the time goes in v6:
time: 62.4 us; the launch traced here: 62.2 us
  Pallas kernels  60.9 us (98%)
  local copies, waits for them, and re-layouts  1.32 us (2%)
    pallas_call x1, Pallas kernels, shards(): pl.pallas_call(kernel, out_shape=jax.ShapeDtypeStruct((B // 2, B), BF16),...  60.9 us
    unnamed x1, local copies, waits for them, and re-layouts  1.32 us

profile of v6, /device:TPU:1, one launch (start us, length us, event | category | flops | bytes accessed | tf_op | source)
XLA Modules:
  0.0 62.2 jit_solution(8617895247232076751)
XLA Ops:
  0.0 60.9 %shard_map.46 = bf16[64,128]{1,0:T(8,128)(2,1)} custom-call(bf16[128,2048]{1,0:T(8,128)(2,1)} %psi.1, bf16[1,128,2048]{2,1,0:T(8,128)(2,1)} %left.1, bf16[1,128,2048]{2,1,0:T(8,128)(2,1)} %right.1, s32[1,1,16]{2,1,0:T(1,128)} %mask.1), custom_call_target="tpu_custom_call" | custom-call | tf_op jit(solution)/shard_map/pallas_call | solution.py:320
  60.9 1.3 %copy.6 = bf16[128,64]{0,1:T(8,128)(2,1)} copy(bf16[128,64]{0,1:T(8,128)(2,1)} %bitcast.1) | data formatting | bytes 32768
